TPU v7x, 32 devices: a whole 2x2x4 slice. The times are simulated.
32 devices in a mesh: tile: 8 (over z, x), grp: 4 (over y, core).
Axes of the slice: x: 2, y: 2, z: 4, core: 2. Of those that a mesh axis runs over, the one named last changes fastest.
Arguments:
- pixels: bfloat16 [8192, 432], P(('tile', 'grp')), may hold values from -25 to 25
- labels: int32 [8192], P(('tile', 'grp')), may hold values from 0 to 63, as said below
- targets: bfloat16 [512, 432], P('grp'), may hold values from -6 to 6
Outputs:
- scores: bfloat16 [8192, 512], P(('tile', 'grp'))
Inputs may be any that keep to these rules, and one draw needn't show every extreme that they name: `labels`: among the 256 pixels of each aligned block (rows b * 256 to (b + 1) * 256 - 1) no cluster occurs more than 8 times; in every draw one cluster occurs exactly 8 times in every block.
All inputs are finite; a program needn't handle non-finite values.
Results may differ from a plain program's by a relative error of at most 0.0024.
Values may be sent and summed in bfloat16 or wider, within the bound.
A program may use at most 128 MiB of HBM per device.

v0:
```python
import jax
import jax.numpy as jnp
from jax import lax
from jax.sharding import PartitionSpec as P

NCLUST = 64
CAP = 8


def local(pixels, labels, targets):
    n_tile = lax.axis_size("tile")
    n_grp = lax.axis_size("grp")
    band_count = pixels.shape[1]
    per_owner = 2 * NCLUST // n_tile
    target_total = targets.shape[0] * n_grp
    clusters = jnp.arange(NCLUST, dtype=jnp.int32)
    member = (labels[:, None] == clusters[None, :]).astype(jnp.int32)
    local_count = jnp.sum(member, axis=0).astype(jnp.float32)
    counts = lax.psum(local_count, ("tile", "grp"))
    place_rank = jnp.sum(jnp.cumsum(member, axis=0) * member, axis=1) - 1
    owner_pair = labels // per_owner
    inner_slot = labels % per_owner
    slot_width = CAP
    target_tile = 2 * owner_pair
    slot_index = (target_tile * per_owner + inner_slot) * slot_width + place_rank
    slot_total = n_tile * per_owner * slot_width
    outgoing = jnp.zeros((slot_total, band_count), jnp.bfloat16).at[slot_index].set(pixels)
    outgoing = outgoing.reshape(n_tile, per_owner * slot_width, band_count)
    arrived = lax.all_to_all(outgoing, "tile", split_axis=0, concat_axis=0, tiled=True)
    grouped = arrived.reshape(n_tile, per_owner, slot_width, band_count)
    gram_sum = jnp.einsum("scwb,scwd->cbd", grouped, grouped, preferred_element_type=jnp.float32)
    first_sums = jnp.sum(grouped, axis=(0, 2), dtype=jnp.float32)
    gram_sum, first_sums = lax.psum((gram_sum, first_sums), "grp")
    own_pair = lax.axis_index("tile") // 2
    own_counts = lax.dynamic_slice_in_dim(counts, own_pair * per_owner, per_owner, 0)
    own_counts = jnp.maximum(own_counts, 1.0)
    centre = first_sums / own_counts[:, None]
    identity = jnp.eye(band_count, dtype=jnp.float32)
    covariance = (
        gram_sum / own_counts[:, None, None]
        - centre[:, :, None] * centre[:, None, :]
        + 0.05 * identity
    )
    factor = jnp.linalg.cholesky(covariance)
    inverse = jax.scipy.linalg.solve_triangular(
        factor, jnp.broadcast_to(identity, factor.shape), lower=True
    )
    whitened = jnp.einsum(
        "tb,cdb->ctd",
        lax.all_gather(targets, "grp", axis=0, tiled=True).astype(jnp.float32),
        inverse,
        precision=lax.Precision.HIGHEST,
    )
    lib_norm = jnp.sum(whitened * whitened, axis=-1)
    centered = grouped.astype(jnp.float32) - centre[None, :, None, :]
    white_pix = jnp.einsum("scwb,cdb->scwd", centered, inverse, precision=lax.Precision.HIGHEST)
    inner_prod = jnp.einsum("scwd,ctd->scwt", white_pix, whitened, precision=lax.Precision.HIGHEST)
    pix_norm = jnp.sum(white_pix * white_pix, axis=-1)
    result = (
        band_count
        * inner_prod
        * inner_prod
        / ((lib_norm[None, :, None, :] + 1e-06) * (pix_norm[:, :, :, None] + 1e-06))
    )
    outbound = result.astype(jnp.bfloat16).reshape(n_tile, per_owner * slot_width, target_total)
    returned = lax.all_to_all(outbound, "tile", split_axis=0, concat_axis=0, tiled=True)
    flat_scores = returned.reshape(slot_total, target_total)
    return flat_scores[slot_index]


def solution(mesh):
    return jax.shard_map(
        local,
        mesh=mesh,
        in_specs=(P(("tile", "grp"), None), P(("tile", "grp")), P("grp", None)),
        out_specs=P(("tile", "grp"), None),
        check_vma=False,
    )
```

profile of v0, /device:TPU:27, one launch (start us, length us, event | category | flops | bytes accessed | tf_op | source)
XLA Modules:
  0.0 2279.1 jit_solution(9850537382942361568)
XLA Ops:
  13.3 25.5 %all_to_all.10 = bf16[8,128,432]{1,2,0:T(8,128)(2,1)S(1)} all-to-all(bf16[8,128,432]{1,2,0:T(8,128)(2,1)S(1)} %copy.111), channel_id=1, replica_groups=mesh['tile'=8,'grp'=4] {'tile'}, dimensions={0} | all-to-all | bytes 1769472 | tf_op jit(solution)/shard_map/all_to_all | solution.py:29
  47.5 40.4 %psum.22 = f32[64]{0:T(128)S(1)} all-reduce(f32[64]{0:T(128)S(1)} %convert_element_type.32), channel_id=1, replica_groups=mesh['tile'=8,'grp'=4] {'tile','grp'}, use_global_device_ids=true, to_apply=%region_6.7 | all-reduce | flops 64 | bytes 512 | tf_op jit(solution)/shard_map/psum | solution.py:19
  91.2 11.3 all_gather.3
  103.7 12.1 psum.23
  115.9 181.6 %all-reduce.5.cloned.1.call-done = f32[16,432,432]{1,2,0:T(8,128)} async-done(((f32[16,432,432]{1,2,0:T(8,128)}), f32[16,432,432]{1,2,0:T(8,128)}) %all-reduce.5.cloned.1.call-update) | async-done | bytes 11943952 | tf_op jit(solution)/shard_map/psum | solution.py:33
  297.5 10.6 subtract_add_fusion
  308.2 16.3 copy.115
  324.5 10.2 fusion.4
  339.9 187.5 %custom-call.35 = f32[16,128,128]{2,1,0:T(8,128)S(1)} custom-call(f32[16,128,128]{2,1,0:T(8,128)S(1)} %cholesky.281), custom_call_target="Cholesky" | custom-call | tf_op jit(solution)/shard_map/jit(cholesky)/cholesky | solution.py:44
  534.5 157.4 %custom-call.36 = f32[16,1,128,128]{2,3,1,0:T(8,128)S(1)} custom-call(f32[16,1,128,128]{3,2,1,0:T(8,128)S(1)} %select_bitcast_fusion.2), custom_call_target="InvertDiagBlocksLowerTriangular" | custom-call | tf_op jit(solution)/shard_map/jit(cholesky)/cholesky | solution.py:44
  702.7 189.1 %custom-call.37 = f32[16,128,128]{2,1,0:T(8,128)} custom-call(f32[16,128,128]{2,1,0:T(8,128)} %cholesky.285), custom_call_target="Cholesky" | custom-call | tf_op jit(solution)/shard_map/jit(cholesky)/cholesky | solution.py:44
  894.7 159.0 %custom-call.38 = f32[16,1,128,128]{2,3,1,0:T(8,128)} custom-call(f32[16,1,128,128]{3,2,1,0:T(8,128)} %get-tuple-element.30), custom_call_target="InvertDiagBlocksLowerTriangular" | custom-call | tf_op jit(solution)/shard_map/jit(cholesky)/cholesky | solution.py:44
  1064.6 189.0 %custom-call.39 = f32[16,128,128]{2,1,0:T(8,128)} custom-call(f32[16,128,128]{2,1,0:T(8,128)} %cholesky.290), custom_call_target="Cholesky" | custom-call | tf_op jit(solution)/shard_map/jit(cholesky)/cholesky | solution.py:44
  1257.3 158.2 %custom-call.40 = f32[16,1,128,128]{2,3,1,0:T(8,128)S(1)} custom-call(f32[16,1,128,128]{3,2,1,0:T(8,128)} %get-tuple-element.28), custom_call_target="InvertDiagBlocksLowerTriangular" | custom-call | tf_op jit(solution)/shard_map/jit(cholesky)/cholesky | solution.py:44
  1420.6 70.4 %custom-call.41 = f32[16,48,48]{2,1,0:T(8,128)S(1)} custom-call(f32[16,48,48]{2,1,0:T(8,128)S(1)} %convolution_subtract_fusion), custom_call_target="Cholesky" | custom-call | tf_op jit(solution)/shard_map/jit(cholesky)/cholesky | solution.py:44
  1492.2 12.5 select_select_fusion
  1505.8 12.0 while.1
  1521.5 630.4 %custom-call.42 = f32[16,4,128,128]{2,3,1,0:T(8,128)} custom-call(f32[16,4,128,128]{3,2,1,0:T(8,128)} %pad_maximum_fusion.3), custom_call_target="InvertDiagBlocksLowerTriangular" | custom-call | tf_op jit(solution)/shard_map/jit(_solve_triangular)/vmap()/triangular_solve | solution.py:45
  2164.6 9.1 fusion.12
  2177.3 12.2 fusion.5
  2195.3 14.7 fusion.29
  2210.1 17.1 multiply_reduce_fusion
  2227.2 12.4 fusion.25
  2246.1 24.1 %all-to-all-done.1 = bf16[8,128,512]{2,1,0:T(8,128)(2,1)S(1)} async-done(((bf16[8,128,512]{2,1,0:T(8,128)(2,1)}), bf16[8,128,512]{2,1,0:T(8,128)(2,1)S(1)}, u32[]{:S(2)}, u32[]{:S(2)}) %all-to-all-start.1) | async-done | bytes 1048608 | tf_op jit(solution)/shard_map/all_to_all | solution.py:66
  (120 shorter events, 113.8 us)
Async XLA Ops:
  6.5 291.0 %all-reduce.5.cloned.1.call-start = ((), (), s32[]{:S(2)}) async-start(), calls=%async_computation.2 | async-start | bytes 28311552 | tf_op jit(solution)/shard_map/psum | solution.py:33
  9.6 3.0 copy-start.19
  39.3 7.2 copy-start.1
  46.5 44.7 %copy-start.14 = (bf16[128,432]{0,1:T(8,128)(2,1)S(1)}, bf16[128,432]{0,1:T(8,128)(2,1)}, u32[]{:S(2)}) copy-start(bf16[128,432]{0,1:T(8,128)(2,1)} %param.5) | copy-start | bytes 331780
  115.9 208.6 %copy-start.10 = (f32[16,432]{1,0:T(8,128)}, f32[16,432]{1,0:T(8,128)S(1)}, u32[]{:S(2)}) copy-start(f32[16,432]{1,0:T(8,128)S(1)} %broadcast_divide_fusion) | copy-start | bytes 82948
  334.7 5.1 copy-start
  1057.6 196.1 %copy-start.3 = (f32[16,128,128]{2,1,0:T(8,128)S(1)}, f32[16,128,128]{2,1,0:T(8,128)}, u32[]{:S(2)}) copy-start(f32[16,128,128]{2,1,0:T(8,128)} %custom-call.37) | copy-start | bytes 3145732
  1257.3 233.7 %copy-start.18 = (pred[48,48]{1,0:T(8,128)(4,1)S(1)}, pred[48,48]{1,0:T(8,128)(4,1)}, u32[]{:S(2)}) copy-start(pred[48,48]{1,0:T(8,128)(4,1)} %iota_compare_fusion.8) | copy-start | bytes 6916
  1257.3 234.7 %copy-start.17 = (f32[16,128]{1,0:T(8,128)S(1)}, f32[16,128]{1,0:T(8,128)}, u32[]{:S(2)}) copy-start(f32[16,128]{1,0:T(8,128)} %get-tuple-element.15) | copy-start | bytes 24580
  1257.3 234.8 %copy-start.15 = (f32[16,128]{1,0:T(8,128)S(1)}, f32[16,128]{1,0:T(8,128)}, u32[]{:S(2)}) copy-start(f32[16,128]{1,0:T(8,128)} %get-tuple-element.13) | copy-start | bytes 24580
  1257.3 234.8 %copy-start.16 = (f32[16,128]{1,0:T(8,128)S(1)}, f32[16,128]{1,0:T(8,128)}, u32[]{:S(2)}) copy-start(f32[16,128]{1,0:T(8,128)} %get-tuple-element.14) | copy-start | bytes 24580
  1257.3 234.9 %copy-start.6 = (pred[432,432]{1,0:T(8,128)(4,1)S(1)}, pred[432,432]{1,0:T(8,128)(4,1)}, u32[]{:S(2)}) copy-start(pred[432,432]{1,0:T(8,128)(4,1)} %iota_compare_fusion.2) | copy-start | bytes 559876
  1492.2 13.6 copy-start.21
  1492.2 13.6 copy-start.4
  1519.2 632.7 %copy-start.9 = (f32[128,432]{0,1:T(8,128)S(1)}, f32[128,432]{0,1:T(8,128)}, u32[]{:S(2)}) copy-start(f32[128,432]{0,1:T(8,128)} %get-tuple-element.34) | copy-start | bytes 663556
  2156.1 4.9 copy-start.5
  2156.1 4.9 copy-start.8
  2164.6 9.1 copy-start.7
  2177.2 12.2 copy-start.13
  2189.4 5.9 copy-start.2
  2189.4 5.9 copy-start.11
  2195.3 14.7 copy-start.12
  2239.6 6.5 copy-start.20
  2240.7 29.5 %all-to-all-start.1 = ((bf16[8,128,512]{2,1,0:T(8,128)(2,1)}), bf16[8,128,512]{2,1,0:T(8,128)(2,1)S(1)}, u32[]{:S(2)}, u32[]{:S(2)}) async-start(bf16[8,128,512]{2,1,0:T(8,128)(2,1)} %bitcast.107), calls=%async_computation.1 | async-start | bytes 2097152 | tf_op jit(solution)/shard_map/all_to_all | solution.py:66
Sparse Core Ops, SparseCore 0:
  46.6 250.8 all-reduce.4
where the time goes:
time: 2290 us; the launch traced here: 2280 us
  other arithmetic  1790 us (78%)
  waiting for transfers between devices  206 us (9%)
  matrix products  119 us (5%)
  blocking collectives  89.3 us (4%)
  local copies, waits for them, and re-layouts  53.8 us (2%)
    another operation x18, other arithmetic, local(): factor = jnp.linalg.cholesky(covariance)  1120 us
    another operation x8, other arithmetic, local(): jax.scipy.linalg.solve_triangular(factor, jnp.broadcast_to(identity, fact...  647 us
    psum x1, waiting for transfers between devices, local(): gram_sum, first_sums = lax.psum((gram_sum, first_sums), 'grp')  182 us
  transfers between devices with their start and end apart: 2, of which 2 were waited for; matrix products, arithmetic and copies ran while one was open for 0% of the time, Pallas kernels for 0%

commit v1 on v0

--- a/solution.py
+++ b/solution.py
@@ -1,13 +1,153 @@
+import functools
+
 import jax
 import jax.numpy as jnp
 from jax import lax
+from jax.experimental import pallas as pl
+from jax.experimental.pallas import tpu as pltpu
 from jax.sharding import PartitionSpec as P
 
 NCLUST = 64
 CAP = 8
-
-
-def local(pixels, labels, targets):
+RIDGE = 0.05
+LIFT = 1.0
+EPS = 1e-06
+STEP = 32
+LANES = 128
+AXES = ("tile", "grp")
+HI = lax.Precision.HIGHEST
+F32 = jnp.float32
+BF16 = jnp.bfloat16
+
+
+def dot_t(a, b, prec=None):
+    return lax.dot_general(a, b, (((1,), (1,)), ((), ())), precision=prec, preferred_element_type=F32)
+
+
+def dot_0(a, b, prec=None):
+    return lax.dot_general(a, b, (((0,), (0,)), ((), ())), precision=prec, preferred_element_type=F32)
+
+
+def dot_n(a, b, prec=None):
+    return lax.dot_general(a, b, (((1,), (0,)), ((), ())), precision=prec, preferred_element_type=F32)
+
+
+def panel_inverse(panels, first):
+    rows, width = panels[0].shape
+    lane = lax.broadcasted_iota(jnp.int32, (rows, width), 1)
+    row = lax.broadcasted_iota(jnp.int32, (rows, width), 0)
+    lane1 = lax.broadcasted_iota(jnp.int32, (1, width), 1)
+    for j in range(rows):
+        at = first + j
+        fresh = []
+        for panel in panels:
+            col = panel[:, at : at + 1]
+            inv = 1.0 / col[j : j + 1, :]
+            norm = jnp.where(lane1 == at, 1.0, panel[j : j + 1, :]) * inv
+            rest = jnp.where(lane == at, 0.0, panel) - col * norm
+            fresh.append(jnp.where(row == j, norm, rest))
+        panels = fresh
+    return panels
+
+
+def invert_all(mats):
+    size = mats[0].shape[0]
+    lane1 = lax.broadcasted_iota(jnp.int32, (1, size), 1)
+    for k in range(size // STEP):
+        lo = k * STEP
+        inside = (lane1 >= lo) & (lane1 < lo + STEP)
+        sign = jnp.where(lane1 < lo, -1.0, jnp.where(inside, 0.0, 1.0))
+        rows = [m[lo : lo + STEP, :] for m in mats]
+        outs = panel_inverse(rows, lo)
+        fresh = []
+        for m, r, w in zip(mats, rows, outs):
+            kept = jnp.where(inside, 0.0, m)
+            upd = kept - dot_0(r * sign, w, HI)
+            parts = [upd[:lo]] * (lo > 0) + [w] + [upd[lo + STEP :]] * (lo + STEP < size)
+            fresh.append(jnp.concatenate(parts, axis=0))
+        mats = fresh
+    return mats
+
+
+def cluster_gram(x, bands):
+    size = x.shape[0]
+    gram = dot_t(x, x)
+    valid = x[:, bands : bands + 1].astype(F32)
+    ri = lax.broadcasted_iota(jnp.int32, (size, size), 0)
+    ci = lax.broadcasted_iota(jnp.int32, (size, size), 1)
+    diag = ri == ci
+    valid_row = jnp.sum(jnp.where(diag, valid, 0.0), axis=0, keepdims=True)
+    count = jnp.maximum(jnp.sum(valid), 1.0)
+    share = 1.0 / count
+    mean_r = jnp.sum(gram, axis=0, keepdims=True) * share
+    mean_c = jnp.sum(gram, axis=1, keepdims=True) * share
+    mean = jnp.sum(mean_r) * share
+    mat = (gram - mean_r - mean_c + (mean + LIFT)) * (valid * valid_row) * share
+    mat = mat + jnp.where(diag, RIDGE, 0.0)
+    return mat, valid, count, diag
+
+
+def cluster_scores(x, targets, tnorm, inverse, valid, count, diag, bands):
+    share = 1.0 / count
+    u = dot_t(x, targets)
+    u = (u - jnp.sum(u, axis=0, keepdims=True) * share) * valid
+    z = dot_n(inverse, u, HI)
+    kd = jnp.sum(jnp.where(diag, inverse, 0.0), axis=1, keepdims=True)
+    pix = count * (1.0 - RIDGE * kd) - LIFT / (LIFT + RIDGE)
+    pix = jnp.maximum(pix, 0.0) + EPS
+    lib = (tnorm - jnp.sum(u * z, axis=0, keepdims=True) * share) * (1.0 / RIDGE)
+    lib = jnp.maximum(lib, 0.0) + EPS
+    return z * z * (bands / pix) * (1.0 / lib)
+
+
+def owner_body(bands, owned, x_ref, t_ref, out_ref):
+    slots = x_ref.shape[0]
+    devices = slots // (owned * CAP)
+    width = x_ref.shape[1]
+    xf = x_ref[...].astype(F32).reshape(devices, owned, CAP, width)
+    xs = [xf[:, c].reshape(devices * CAP, width).astype(BF16) for c in range(owned)]
+    grams = [cluster_gram(x, bands) for x in xs]
+    inverses = invert_all([g[0] for g in grams])
+    targets = t_ref[...]
+    tf = targets.astype(F32)
+    tnorm = dot_t(jnp.ones((8, width), F32), tf * tf, HI)[0:1]
+    res = []
+    for x, g, inv in zip(xs, grams, inverses):
+        s = cluster_scores(x, targets, tnorm, inv, g[1], g[2], g[3], bands)
+        res.append(s.reshape(devices, 1, CAP, s.shape[1]))
+    full = jnp.concatenate(res, axis=1)
+    out_ref[...] = full.reshape(slots, full.shape[-1]).astype(BF16)
+
+
+def narrow(pixels, labels, targets):
+    devices = lax.axis_size("tile") * lax.axis_size("grp")
+    owned = NCLUST // devices
+    bands = pixels.shape[1]
+    width = -(-(bands + 1) // LANES) * LANES
+    slots = NCLUST * CAP
+    clusters = jnp.arange(NCLUST, dtype=jnp.int32)
+    member = (labels[:, None] == clusters[None, :]).astype(jnp.int32)
+    rank = jnp.sum(jnp.cumsum(member, axis=0) * member, axis=1) - 1
+    index = labels * CAP + rank
+    onehot = (index[:, None] == jnp.arange(slots, dtype=jnp.int32)[None, :]).astype(BF16)
+    ones = jnp.ones((pixels.shape[0], 1), BF16)
+    wide = jnp.concatenate([pixels, ones, jnp.zeros((pixels.shape[0], width - bands - 1), BF16)], axis=1)
+    outgoing = dot_0(onehot, wide).astype(BF16)
+    arrived = lax.all_to_all(outgoing, AXES, split_axis=0, concat_axis=0, tiled=True)
+    library = lax.all_gather(targets, "grp", axis=0, tiled=True)
+    library = jnp.pad(library, ((0, 0), (0, width - bands)))
+    out = pl.pallas_call(
+        functools.partial(owner_body, bands, owned),
+        out_shape=jax.ShapeDtypeStruct((slots, library.shape[0]), BF16),
+        in_specs=[pl.BlockSpec(memory_space=pltpu.VMEM)] * 2,
+        out_specs=pl.BlockSpec(memory_space=pltpu.VMEM),
+        compiler_params=pltpu.CompilerParams(vmem_limit_bytes=60 * 1024 * 1024),
+    )(arrived, library)
+    returned = lax.all_to_all(out, AXES, split_axis=0, concat_axis=0, tiled=True)
+    return dot_n(onehot, returned).astype(BF16)
+
+
+def wide_cluster(pixels, labels, targets):
     n_tile = lax.axis_size("tile")
     n_grp = lax.axis_size("grp")
     band_count = pixels.shape[1]
@@ -68,6 +208,13 @@
     return flat_scores[slot_index]
 
 
+def local(pixels, labels, targets):
+    devices = lax.axis_size("tile") * lax.axis_size("grp")
+    if NCLUST % devices == 0 and devices * CAP <= pixels.shape[1]:
+        return narrow(pixels, labels, targets)
+    return wide_cluster(pixels, labels, targets)
+
+
 def solution(mesh):
     return jax.shard_map(
         local,

time: 2290 us -> 78.4 us (0.03)
  the two profiles are of different devices: /device:TPU:27 before, /device:TPU:0 now
where the time goes in v1:
time: 78.4 us; the launch traced here: 78 us
  Pallas kernels  31.4 us (40%)
  blocking collectives  29.4 us (38%)
  starting transfers between devices  7.33 us (9%)
  waiting for transfers between devices  3.86 us (5%)
  local copies, waits for them, and re-layouts  2.79 us (4%)
  matrix products  2.4 us (3%)
    pallas_call x1, Pallas kernels, narrow(): pl.pallas_call(functools.partial(owner_body, bands, owned), out_shape=jax...  31.4 us
    all_to_all x1, blocking collectives, narrow(): lax.all_to_all(out, AXES, split_axis=0, concat_axis=0, tiled=True)  18.6 us
    all_gather x1, blocking collectives, narrow(): library = lax.all_gather(targets, 'grp', axis=0, tiled=True)  10.8 us
    all_to_all x1, starting transfers between devices, narrow(): lax.all_to_all(outgoing, AXES, split_axis=0, concat_axis=0, tiled=True)  7.33 us
    all_to_all x1, waiting for transfers between devices, narrow(): lax.all_to_all(outgoing, AXES, split_axis=0, concat_axis=0, tiled=True)  3.86 us
    unnamed x9, local copies, waits for them, and re-layouts  1.61 us
  transfers between devices with their start and end apart: 1, of which 1 were waited for; matrix products, arithmetic and copies ran while one was open for 1% of the time, Pallas kernels for 0%

profile of v1, /device:TPU:0, one launch (start us, length us, event | category | flops | bytes accessed | tf_op | source)
XLA Modules:
  0.0 78.0 jit_solution(1757311840443727404)
XLA Ops:
  0.0 0.0 copy-start.2
  0.0 0.0 copy-start.3
  0.0 0.7 copy-done.2
  0.7 0.6 reduce-window.6
  1.3 0.2 slice_reduce_fusion
  1.5 0.1 fusion.10
  1.7 0.1 pad.7.clone
  1.7 0.1 pad.6.clone
  1.8 0.0 copy-done.3
  1.8 1.3 %convolution_convert_fusion = bf16[512,512]{1,0:T(8,128)(2,1)} fusion(bf16[256,432]{0,1:T(8,128)(2,1)S(1)} %copy-done.3, s32[256]{0:T(256)S(1)} %add_add_fusion, bf16[512]{0:T(512)(128)(2,1)S(1)} %pad.7.clone, bf16[512]{0:T(512)(128)(2,1)S(1)} %pad.6.clone), kind=kOutput, calls=%fused_computation | convolution fusion | flops 135528448 | bytes 748544 | tf_op jit(solution)/shard_map/dot_general | solution.py:28
  3.2 0.0 copy-start.1
  3.2 7.3 %all-to-all-start = ((bf16[32,16,512]{2,1,0:T(8,128)(2,1)}), bf16[32,16,512]{2,1,0:T(8,128)(2,1)S(1)}, u32[]{:S(2)}, u32[]{:S(2)}) async-start(bf16[32,16,512]{2,1,0:T(8,128)(2,1)} %bitcast.2), calls=%async_computation | async-start | bytes 1048576 | tf_op jit(solution)/shard_map/all_to_all | solution.py:136
  10.5 0.0 copy-done.1
  10.5 0.1 copy.6
  10.6 10.8 %all_gather.3 = bf16[512,432]{1,0:T(8,128)(2,1)S(1)} all-gather(bf16[128,432]{1,0:T(8,128)(2,1)S(1)} %copy.6), channel_id=1, replica_groups=mesh['tile'=8,'grp'=4] {'grp'}, dimensions={0}, use_global_device_ids=true | all-gather | bytes 552960 | tf_op jit(solution)/shard_map/all_gather | solution.py:137
  21.4 0.8 %pad.4.t_ref = bf16[512,512]{1,0:T(8,128)(2,1)} pad(bf16[512,432]{1,0:T(8,128)(2,1)S(1)} %all_gather.3, bf16[]{:T(256)} %constant.15.clone.1), padding=0_0x0_80 | pad | bytes 966658 | tf_op jit(solution)/shard_map/jit(_pad)/pad | solution.py:138
  22.3 3.9 %all-to-all-done = bf16[32,16,512]{2,1,0:T(8,128)(2,1)S(1)} async-done(((bf16[32,16,512]{2,1,0:T(8,128)(2,1)}), bf16[32,16,512]{2,1,0:T(8,128)(2,1)S(1)}, u32[]{:S(2)}, u32[]{:S(2)}) %all-to-all-start) | async-done | bytes 524320 | tf_op jit(solution)/shard_map/all_to_all | solution.py:136
  26.1 0.0 copy-start
  26.1 0.8 %copy-done = bf16[32,16,512]{2,1,0:T(8,128)(2,1)} copy-done((bf16[32,16,512]{2,1,0:T(8,128)(2,1)}, bf16[32,16,512]{2,1,0:T(8,128)(2,1)S(1)}, u32[]{:S(2)}) %copy-start) | copy-done | bytes 524312
  26.9 31.4 %shard_map.37 = bf16[512,512]{1,0:T(8,128)(2,1)} custom-call(bf16[512,512]{1,0:T(8,128)(2,1)} %bitcast.22, bf16[512,512]{1,0:T(8,128)(2,1)} %pad.4.t_ref), custom_call_target="tpu_custom_call" | custom-call | tf_op jit(solution)/shard_map/pallas_call | solution.py:139
  58.3 18.6 %all_to_all.23 = bf16[32,16,512]{2,1,0:T(8,128)(2,1)S(1)} all-to-all(bf16[32,16,512]{2,1,0:T(8,128)(2,1)} %bitcast.23), channel_id=1, replica_groups=mesh['tile'=8,'grp'=4] {'tile','grp'}, dimensions={0} | all-to-all | bytes 1048576 | tf_op jit(solution)/shard_map/all_to_all | solution.py:146
  77.0 1.1 %convolution_convert_fusion.1 = bf16[256,512]{1,0:T(8,128)(2,1)} fusion(bf16[512,512]{1,0:T(8,128)(2,1)S(1)} %bitcast.24, s32[256]{0:T(256)S(1)} %add_add_fusion), kind=kOutput, calls=%fused_computation.1 | convolution fusion | flops 134479872 | bytes 787456 | tf_op jit(solution)/shard_map/dot_general | solution.py:32
  (5 shorter events, 0.1 us)
Async XLA Ops:
  0.0 0.7 copy-start.2
  0.0 1.8 %copy-start.3 = (bf16[256,432]{0,1:T(8,128)(2,1)S(1)}, bf16[256,432]{0,1:T(8,128)(2,1)}, u32[]{:S(2)}) copy-start(bf16[256,432]{0,1:T(8,128)(2,1)} %param.3) | copy-start | bytes 663556
  3.2 7.3 %copy-start.1 = (bf16[128,432]{0,1:T(8,128)(2,1)S(1)}, bf16[128,432]{0,1:T(8,128)(2,1)}, u32[]{:S(2)}) copy-start(bf16[128,432]{0,1:T(8,128)(2,1)} %param.5) | copy-start | bytes 331780
  3.2 22.9 %all-to-all-start = ((bf16[32,16,512]{2,1,0:T(8,128)(2,1)}), bf16[32,16,512]{2,1,0:T(8,128)(2,1)S(1)}, u32[]{:S(2)}, u32[]{:S(2)}) async-start(bf16[32,16,512]{2,1,0:T(8,128)(2,1)} %bitcast.2), calls=%async_computation | async-start | bytes 1048576 | tf_op jit(solution)/shard_map/all_to_all | solution.py:136
  26.1 0.8 %copy-start = (bf16[32,16,512]{2,1,0:T(8,128)(2,1)}, bf16[32,16,512]{2,1,0:T(8,128)(2,1)S(1)}, u32[]{:S(2)}) copy-start(bf16[32,16,512]{2,1,0:T(8,128)(2,1)S(1)} %all-to-all-done) | copy-start | bytes 1572868

commit v2 on v1

--- a/solution.py
+++ b/solution.py
@@ -14,7 +14,7 @@
 EPS = 1e-06
 STEP = 32
 LANES = 128
-AXES = ("tile", "grp")
+MESH = pl.DeviceIdType.MESH
 HI = lax.Precision.HIGHEST
 F32 = jnp.float32
 BF16 = jnp.bfloat16
@@ -100,51 +100,150 @@
     return z * z * (bands / pix) * (1.0 / lib)
 
 
-def owner_body(bands, owned, x_ref, t_ref, out_ref):
-    slots = x_ref.shape[0]
-    devices = slots // (owned * CAP)
-    width = x_ref.shape[1]
-    xf = x_ref[...].astype(F32).reshape(devices, owned, CAP, width)
+def slot_of(lab_row, slots):
+    count = lab_row.shape[1]
+    ri = lax.broadcasted_iota(jnp.int32, (count, count), 0)
+    ci = lax.broadcasted_iota(jnp.int32, (count, count), 1)
+    lab_row = lab_row.astype(F32)
+    lab_col = jnp.sum(jnp.where(ri == ci, lab_row, 0.0), axis=1, keepdims=True)
+    same = jnp.where(lab_row == lab_col, 1.0, 0.0)
+    rank_col = jnp.sum(jnp.where(ci < ri, same, 0.0), axis=1, keepdims=True)
+    rank_row = jnp.sum(jnp.where(ri < ci, same, 0.0), axis=0, keepdims=True)
+    idx_col = lab_col * CAP + rank_col
+    idx_row = lab_row * CAP + rank_row
+    across = lax.broadcasted_iota(jnp.int32, (count, slots), 1).astype(F32)
+    down = lax.broadcasted_iota(jnp.int32, (slots, count), 0).astype(F32)
+    take = jnp.where(across == idx_col, 1.0, 0.0).astype(BF16)
+    put = jnp.where(down == idx_row, 1.0, 0.0).astype(BF16)
+    return take, put
+
+
+def step_body(
+    bands, owned, n_tile, n_grp,
+    lab_ref, pix_ref, tgt_ref, out_ref,
+    wide, outgoing, arrived, mine, library, outbound, returned, take_ref,
+    send_a, recv_a, send_t, recv_t, send_b, recv_b,
+):
+    devices = n_tile * n_grp
+    group = owned * CAP
+    slots = devices * group
+    width = wide.shape[1]
+    tile = lax.axis_index("tile")
+    grp = lax.axis_index("grp")
+    me = tile * n_grp + grp
+
+    def place(r):
+        other = lax.rem(me + r, devices)
+        return (lax.div(other, n_grp), lax.rem(other, n_grp)), other
+
+    barrier = pltpu.get_barrier_semaphore()
+
+    def greet(r, _):
+        pl.semaphore_signal(barrier, inc=1, device_id=place(r)[0], device_id_type=MESH)
+        return 0
+
+    lax.fori_loop(1, devices, greet, 0)
+
+    wide[...] = jnp.ones_like(wide)
+    wide[:, :bands] = pix_ref[...]
+    mine[...] = jnp.zeros_like(mine)
+    mine[:, :bands] = tgt_ref[...]
+    take, put = slot_of(lab_ref[...], slots)
+    take_ref[...] = take
+    outgoing[...] = dot_n(put, wide[...]).astype(BF16).reshape(devices, group, width)
+    pl.semaphore_wait(barrier, devices - 1)
+
+    def ship(src, dst, sends, recvs, r):
+        where, other = place(r)
+        return pltpu.make_async_remote_copy(
+            src_ref=src.at[other], dst_ref=dst.at[me],
+            send_sem=sends.at[r], recv_sem=recvs.at[r],
+            device_id=where, device_id_type=MESH,
+        )
+
+    def lend(r):
+        return pltpu.make_async_remote_copy(
+            src_ref=mine, dst_ref=library.at[grp],
+            send_sem=send_t.at[r], recv_sem=recv_t.at[r],
+            device_id=(tile, lax.rem(grp + r, n_grp)), device_id_type=MESH,
+        )
+
+    def start_a(r, _):
+        ship(outgoing, arrived, send_a, recv_a, r).start()
+        return 0
+
+    def wait_a(r, _):
+        ship(outgoing, arrived, send_a, recv_a, r).wait()
+        return 0
+
+    def start_b(r, _):
+        ship(outbound, returned, send_b, recv_b, r).start()
+        return 0
+
+    def wait_b(r, _):
+        ship(outbound, returned, send_b, recv_b, r).wait()
+        return 0
+
+    lax.fori_loop(1, devices, start_a, 0)
+    for r in range(1, n_grp):
+        lend(r).start()
+    arrived[me] = outgoing[me]
+    library[grp] = mine[...]
+    lax.fori_loop(1, devices, wait_a, 0)
+
+    xf = arrived[...].astype(F32).reshape(devices, owned, CAP, width)
     xs = [xf[:, c].reshape(devices * CAP, width).astype(BF16) for c in range(owned)]
     grams = [cluster_gram(x, bands) for x in xs]
     inverses = invert_all([g[0] for g in grams])
-    targets = t_ref[...]
+    for r in range(1, n_grp):
+        lend(r).wait()
+    targets = library[...].reshape(n_grp * mine.shape[0], width)
     tf = targets.astype(F32)
     tnorm = dot_t(jnp.ones((8, width), F32), tf * tf, HI)[0:1]
     res = []
     for x, g, inv in zip(xs, grams, inverses):
         s = cluster_scores(x, targets, tnorm, inv, g[1], g[2], g[3], bands)
         res.append(s.reshape(devices, 1, CAP, s.shape[1]))
-    full = jnp.concatenate(res, axis=1)
-    out_ref[...] = full.reshape(slots, full.shape[-1]).astype(BF16)
+    full = jnp.concatenate(res, axis=1).reshape(devices, group, targets.shape[0])
+    outbound[...] = full.astype(BF16)
+    lax.fori_loop(1, devices, start_b, 0)
+    returned[me] = outbound[me]
+    lax.fori_loop(1, devices, wait_b, 0)
+    out_ref[...] = dot_n(take_ref[...], returned[...].reshape(slots, targets.shape[0])).astype(BF16)
 
 
 def narrow(pixels, labels, targets):
-    devices = lax.axis_size("tile") * lax.axis_size("grp")
+    n_tile, n_grp = lax.axis_size("tile"), lax.axis_size("grp")
+    devices = n_tile * n_grp
     owned = NCLUST // devices
-    bands = pixels.shape[1]
+    group = owned * CAP
+    rows, bands = pixels.shape
     width = -(-(bands + 1) // LANES) * LANES
-    slots = NCLUST * CAP
-    clusters = jnp.arange(NCLUST, dtype=jnp.int32)
-    member = (labels[:, None] == clusters[None, :]).astype(jnp.int32)
-    rank = jnp.sum(jnp.cumsum(member, axis=0) * member, axis=1) - 1
-    index = labels * CAP + rank
-    onehot = (index[:, None] == jnp.arange(slots, dtype=jnp.int32)[None, :]).astype(BF16)
-    ones = jnp.ones((pixels.shape[0], 1), BF16)
-    wide = jnp.concatenate([pixels, ones, jnp.zeros((pixels.shape[0], width - bands - 1), BF16)], axis=1)
-    outgoing = dot_0(onehot, wide).astype(BF16)
-    arrived = lax.all_to_all(outgoing, AXES, split_axis=0, concat_axis=0, tiled=True)
-    library = lax.all_gather(targets, "grp", axis=0, tiled=True)
-    library = jnp.pad(library, ((0, 0), (0, width - bands)))
-    out = pl.pallas_call(
-        functools.partial(owner_body, bands, owned),
-        out_shape=jax.ShapeDtypeStruct((slots, library.shape[0]), BF16),
-        in_specs=[pl.BlockSpec(memory_space=pltpu.VMEM)] * 2,
-        out_specs=pl.BlockSpec(memory_space=pltpu.VMEM),
-        compiler_params=pltpu.CompilerParams(vmem_limit_bytes=60 * 1024 * 1024),
-    )(arrived, library)
-    returned = lax.all_to_all(out, AXES, split_axis=0, concat_axis=0, tiled=True)
-    return dot_n(onehot, returned).astype(BF16)
+    total = targets.shape[0] * n_grp
+    vmem = pl.BlockSpec(memory_space=pltpu.VMEM)
+    dma = pltpu.SemaphoreType.DMA
+    return pl.pallas_call(
+        functools.partial(step_body, bands, owned, n_tile, n_grp),
+        out_shape=jax.ShapeDtypeStruct((rows, total), BF16),
+        in_specs=[vmem] * 3,
+        out_specs=vmem,
+        scratch_shapes=[
+            pltpu.VMEM((rows, width), BF16),
+            pltpu.VMEM((devices, group, width), BF16),
+            pltpu.VMEM((devices, group, width), BF16),
+            pltpu.VMEM((targets.shape[0], width), BF16),
+            pltpu.VMEM((n_grp, targets.shape[0], width), BF16),
+            pltpu.VMEM((devices, group, total), BF16),
+            pltpu.VMEM((devices, group, total), BF16),
+            pltpu.VMEM((rows, NCLUST * CAP), BF16),
+            dma((devices,)), dma((devices,)),
+            dma((n_grp,)), dma((n_grp,)),
+            dma((devices,)), dma((devices,)),
+        ],
+        compiler_params=pltpu.CompilerParams(
+            collective_id=0, has_side_effects=True, vmem_limit_bytes=60 * 1024 * 1024
+        ),
+    )(labels.reshape(1, rows), pixels, targets)
 
 
 def wide_cluster(pixels, labels, targets):

time: 78.4 us -> 67.6 us (0.86)
  the two profiles are of different devices: /device:TPU:0 before, /device:TPU:27 now
where the time goes in v2:
time: 67.6 us; the launch traced here: 67.4 us
  Pallas kernels  63.2 us (93%)
  local copies, waits for them, and re-layouts  4.21 us (6%)
    pallas_call x1, Pallas kernels, narrow(): pl.pallas_call(functools.partial(step_body, bands, owned, n_tile, n_grp),...  63.2 us
    unnamed x5, local copies, waits for them, and re-layouts  4.21 us

profile of v2, /device:TPU:27, one launch (start us, length us, event | category | flops | bytes accessed | tf_op | source)
XLA Modules:
  0.0 67.4 jit_solution(1007820342922367070)
XLA Ops:
  0.0 0.0 copy-start
  0.0 1.7 %copy.5.tgt_ref = bf16[128,432]{1,0:T(8,128)(2,1)} copy(bf16[128,432]{0,1:T(8,128)(2,1)} %param.5) | data formatting | bytes 221184 | tf_op args[2]
  1.7 0.0 copy-done
  1.7 0.8 %copy.4.pix_ref = bf16[256,432]{1,0:T(8,128)(2,1)} copy(bf16[256,432]{0,1:T(8,128)(2,1)S(1)} %copy-done) | data formatting | bytes 442368 | tf_op args[0]
  2.5 63.2 %shard_map.37 = bf16[256,512]{1,0:T(8,128)(2,1)} custom-call(s32[1,256]{1,0:T(1,128)} %bitcast.1, bf16[256,432]{1,0:T(8,128)(2,1)} %copy.4.pix_ref, bf16[128,432]{1,0:T(8,128)(2,1)} %copy.5.tgt_ref), custom_call_target="tpu_custom_call" | custom-call | tf_op jit(solution)/shard_map/pallas_call | solution.py:225
  65.7 1.7 %copy.7 = bf16[256,512]{1,0:T(8,128)(2,1)} copy(bf16[256,512]{1,0:T(8,128)(2,1)} %shard_map.37) | data formatting | bytes 524288
Async XLA Ops:
  0.0 1.7 %copy-start = (bf16[256,432]{0,1:T(8,128)(2,1)S(1)}, bf16[256,432]{0,1:T(8,128)(2,1)}, u32[]{:S(2)}) copy-start(bf16[256,432]{0,1:T(8,128)(2,1)} %param.3) | copy-start | bytes 663556

commit v3 on v2

--- a/solution.py
+++ b/solution.py
@@ -12,8 +12,10 @@
 RIDGE = 0.05
 LIFT = 1.0
 EPS = 1e-06
-STEP = 32
+STEP = 64
 LANES = 128
+SUB = 8
+PIV = 4
 MESH = pl.DeviceIdType.MESH
 HI = lax.Precision.HIGHEST
 F32 = jnp.float32
@@ -32,22 +34,64 @@
     return lax.dot_general(a, b, (((1,), (0,)), ((), ())), precision=prec, preferred_element_type=F32)
 
 
+def pivot_inverse(e):
+    r = 1.0 / (e[0][0] * e[1][1] - e[0][1] * e[0][1])
+    i00, i01, i11 = e[1][1] * r, -e[0][1] * r, e[0][0] * r
+    x00 = i00 * e[0][2] + i01 * e[1][2]
+    x01 = i00 * e[0][3] + i01 * e[1][3]
+    x10 = i01 * e[0][2] + i11 * e[1][2]
+    x11 = i01 * e[0][3] + i11 * e[1][3]
+    s00 = e[2][2] - (e[0][2] * x00 + e[1][2] * x10)
+    s01 = e[2][3] - (e[0][2] * x01 + e[1][2] * x11)
+    s11 = e[3][3] - (e[0][3] * x01 + e[1][3] * x11)
+    q = 1.0 / (s00 * s11 - s01 * s01)
+    t00, t01, t11 = s11 * q, -s01 * q, s00 * q
+    y00 = -(x00 * t00 + x01 * t01)
+    y01 = -(x00 * t01 + x01 * t11)
+    y10 = -(x10 * t00 + x11 * t01)
+    y11 = -(x10 * t01 + x11 * t11)
+    n00 = i00 - (y00 * x00 + y01 * x01)
+    n01 = i01 - (y00 * x10 + y01 * x11)
+    n11 = i11 - (y10 * x10 + y11 * x11)
+    return [[n00, n01, y00, y01], [n01, n11, y10, y11], [y00, y10, t00, t01], [y01, y11, t01, t11]]
+
+
+def panel_step(tiles, first, j):
+    rows = tiles[0].shape[0]
+    at = first + j
+    home, off = at // LANES, at % LANES
+    group = j // SUB * SUB
+    lane8 = lax.broadcasted_iota(jnp.int32, (SUB, LANES), 1)
+    lanes = lax.broadcasted_iota(jnp.int32, (rows, LANES), 1)
+    sub8 = lax.broadcasted_iota(jnp.int32, (SUB, LANES), 0)
+    cols = [jnp.broadcast_to(tiles[home][:, off + c : off + c + 1], (rows, LANES)) for c in range(PIV)]
+    spread = lambda v, a: jnp.broadcast_to(v[j + a : j + a + 1, :], (SUB, LANES))
+    inv = pivot_inverse([[spread(cols[c], a) for c in range(PIV)] for a in range(PIV)])
+    fresh = []
+    for t, tile in enumerate(tiles):
+        src = [spread(tile, c) for c in range(PIV)]
+        kept = tile
+        if t == home:
+            block = (lane8 >= off) & (lane8 < off + PIV)
+            src = [jnp.where(block, jnp.where(lane8 == off + c, 1.0, 0.0), v) for c, v in enumerate(src)]
+            kept = jnp.where((lanes >= off) & (lanes < off + PIV), 0.0, tile)
+        norm = [(inv[a][0] * src[0] + inv[a][1] * src[1]) + (inv[a][2] * src[2] + inv[a][3] * src[3]) for a in range(PIV)]
+        wide = [jnp.concatenate([v] * (rows // SUB), axis=0) for v in norm]
+        rest = kept - ((cols[0] * wide[0] + cols[1] * wide[1]) + (cols[2] * wide[2] + cols[3] * wide[3]))
+        own = rest[group : group + SUB]
+        for a in range(PIV):
+            own = jnp.where(sub8 == j - group + a, norm[a], own)
+        parts = [rest[:group]] * (group > 0) + [own] + [rest[group + SUB :]] * (group + SUB < rows)
+        fresh.append(jnp.concatenate(parts, axis=0) if len(parts) > 1 else parts[0])
+    return fresh
+
+
 def panel_inverse(panels, first):
     rows, width = panels[0].shape
-    lane = lax.broadcasted_iota(jnp.int32, (rows, width), 1)
-    row = lax.broadcasted_iota(jnp.int32, (rows, width), 0)
-    lane1 = lax.broadcasted_iota(jnp.int32, (1, width), 1)
-    for j in range(rows):
-        at = first + j
-        fresh = []
-        for panel in panels:
-            col = panel[:, at : at + 1]
-            inv = 1.0 / col[j : j + 1, :]
-            norm = jnp.where(lane1 == at, 1.0, panel[j : j + 1, :]) * inv
-            rest = jnp.where(lane == at, 0.0, panel) - col * norm
-            fresh.append(jnp.where(row == j, norm, rest))
-        panels = fresh
-    return panels
+    split = [[p[:, t : t + LANES] for t in range(0, width, LANES)] for p in panels]
+    for j in range(0, rows, PIV):
+        split = [panel_step(tiles, first, j) for tiles in split]
+    return [jnp.concatenate(tiles, axis=1) for tiles in split]
 
 
 def invert_all(mats):

time: 67.6 us -> 56.9 us (0.84)
  Pallas kernels: 63.2 us -> 52.5 us
    pallas_call x1, Pallas kernels: 63.2 us -> 52.5 us  [narrow(): pl.pallas_call(functools.partial(step_body, bands, owned, n_tile, n_grp),...]
where the time goes in v3:
time: 56.9 us; the launch traced here: 56.8 us
  Pallas kernels  52.5 us (92%)
  local copies, waits for them, and re-layouts  4.21 us (7%)
    pallas_call x1, Pallas kernels, narrow(): pl.pallas_call(functools.partial(step_body, bands, owned, n_tile, n_grp),...  52.5 us
    unnamed x5, local copies, waits for them, and re-layouts  4.21 us

profile of v3, /device:TPU:27, one launch (start us, length us, event | category | flops | bytes accessed | tf_op | source)
XLA Modules:
  0.0 56.8 jit_solution(12259465050898373817)
XLA Ops:
  0.0 0.0 copy-start
  0.0 1.7 %copy.5.tgt_ref = bf16[128,432]{1,0:T(8,128)(2,1)} copy(bf16[128,432]{0,1:T(8,128)(2,1)} %param.5) | data formatting | bytes 221184 | tf_op args[2]
  1.7 0.0 copy-done
  1.7 0.8 %copy.4.pix_ref = bf16[256,432]{1,0:T(8,128)(2,1)} copy(bf16[256,432]{0,1:T(8,128)(2,1)S(1)} %copy-done) | data formatting | bytes 442368 | tf_op args[0]
  2.5 52.5 %shard_map.37 = bf16[256,512]{1,0:T(8,128)(2,1)} custom-call(s32[1,256]{1,0:T(1,128)} %bitcast.1, bf16[256,432]{1,0:T(8,128)(2,1)} %copy.4.pix_ref, bf16[128,432]{1,0:T(8,128)(2,1)} %copy.5.tgt_ref), custom_call_target="tpu_custom_call" | custom-call | tf_op jit(solution)/shard_map/pallas_call | solution.py:269
  55.1 1.7 %copy.7 = bf16[256,512]{1,0:T(8,128)(2,1)} copy(bf16[256,512]{1,0:T(8,128)(2,1)} %shard_map.37) | data formatting | bytes 524288
Async XLA Ops:
  0.0 1.7 %copy-start = (bf16[256,432]{0,1:T(8,128)(2,1)S(1)}, bf16[256,432]{0,1:T(8,128)(2,1)}, u32[]{:S(2)}) copy-start(bf16[256,432]{0,1:T(8,128)(2,1)} %param.3) | copy-start | bytes 663556

commit v4 on v3

--- a/solution.py
+++ b/solution.py
@@ -32,6 +32,26 @@
 
 def dot_n(a, b, prec=None):
     return lax.dot_general(a, b, (((1,), (0,)), ((), ())), precision=prec, preferred_element_type=F32)
+
+
+def halves(v):
+    big = v.astype(BF16)
+    return big, (v - big.astype(F32)).astype(BF16)
+
+
+def thirds(v):
+    big, rest = v.astype(BF16), v
+    rest = rest - big.astype(F32)
+    mid = rest.astype(BF16)
+    return big, mid, (rest - mid.astype(F32)).astype(BF16)
+
+
+def outer_update(a, b):
+    a1, a2, a3 = thirds(a)
+    b1, b2, b3 = thirds(b)
+    left = jnp.concatenate([a1, a1, a2, a1, a2, a3], axis=0)
+    right = jnp.concatenate([b1, b2, b1, b3, b2, b1], axis=0)
+    return dot_0(left, right)
 
 
 def pivot_inverse(e):
@@ -94,11 +114,13 @@
     return [jnp.concatenate(tiles, axis=1) for tiles in split]
 
 
-def invert_all(mats):
+def invert_all(mats, midway):
     size = mats[0].shape[0]
     lane1 = lax.broadcasted_iota(jnp.int32, (1, size), 1)
     for k in range(size // STEP):
         lo = k * STEP
+        if k == size // STEP // 2:
+            midway()
         inside = (lane1 >= lo) & (lane1 < lo + STEP)
         sign = jnp.where(lane1 < lo, -1.0, jnp.where(inside, 0.0, 1.0))
         rows = [m[lo : lo + STEP, :] for m in mats]
@@ -106,7 +128,7 @@
         fresh = []
         for m, r, w in zip(mats, rows, outs):
             kept = jnp.where(inside, 0.0, m)
-            upd = kept - dot_0(r * sign, w, HI)
+            upd = kept - outer_update(r * sign, w)
             parts = [upd[:lo]] * (lo > 0) + [w] + [upd[lo + STEP :]] * (lo + STEP < size)
             fresh.append(jnp.concatenate(parts, axis=0))
         mats = fresh
@@ -131,11 +153,10 @@
     return mat, valid, count, diag
 
 
-def cluster_scores(x, targets, tnorm, inverse, valid, count, diag, bands):
+def cluster_scores(u, tnorm, inverse, count, diag, bands):
     share = 1.0 / count
-    u = dot_t(x, targets)
-    u = (u - jnp.sum(u, axis=0, keepdims=True) * share) * valid
-    z = dot_n(inverse, u, HI)
+    (k1, k2), (u1, u2) = halves(inverse), halves(u)
+    z = dot_n(k1, u1) + (dot_n(k1, u2) + dot_n(k2, u1))
     kd = jnp.sum(jnp.where(diag, inverse, 0.0), axis=1, keepdims=True)
     pix = count * (1.0 - RIDGE * kd) - LIFT / (LIFT + RIDGE)
     pix = jnp.maximum(pix, 0.0) + EPS
@@ -172,6 +193,7 @@
     group = owned * CAP
     slots = devices * group
     width = wide.shape[1]
+    total = outbound.shape[2]
     tile = lax.axis_index("tile")
     grp = lax.axis_index("grp")
     me = tile * n_grp + grp
@@ -238,22 +260,29 @@
     xf = arrived[...].astype(F32).reshape(devices, owned, CAP, width)
     xs = [xf[:, c].reshape(devices * CAP, width).astype(BF16) for c in range(owned)]
     grams = [cluster_gram(x, bands) for x in xs]
-    inverses = invert_all([g[0] for g in grams])
-    for r in range(1, n_grp):
-        lend(r).wait()
-    targets = library[...].reshape(n_grp * mine.shape[0], width)
-    tf = targets.astype(F32)
-    tnorm = dot_t(jnp.ones((8, width), F32), tf * tf, HI)[0:1]
+    held = {}
+
+    def midway():
+        for r in range(1, n_grp):
+            lend(r).wait()
+        targets = library[...].reshape(n_grp * mine.shape[0], width)
+        tf = targets.astype(F32)
+        held["norm"] = dot_t(jnp.ones((8, width), F32), tf * tf, HI)[0:1]
+        for c, (x, g) in enumerate(zip(xs, grams)):
+            u = dot_t(x, targets)
+            held[c] = (u - jnp.sum(u, axis=0, keepdims=True) * (1.0 / g[2])) * g[1]
+
+    inverses = invert_all([g[0] for g in grams], midway)
     res = []
-    for x, g, inv in zip(xs, grams, inverses):
-        s = cluster_scores(x, targets, tnorm, inv, g[1], g[2], g[3], bands)
+    for c, (g, inv) in enumerate(zip(grams, inverses)):
+        s = cluster_scores(held[c], held["norm"], inv, g[2], g[3], bands)
         res.append(s.reshape(devices, 1, CAP, s.shape[1]))
-    full = jnp.concatenate(res, axis=1).reshape(devices, group, targets.shape[0])
+    full = jnp.concatenate(res, axis=1).reshape(devices, group, total)
     outbound[...] = full.astype(BF16)
     lax.fori_loop(1, devices, start_b, 0)
     returned[me] = outbound[me]
     lax.fori_loop(1, devices, wait_b, 0)
-    out_ref[...] = dot_n(take_ref[...], returned[...].reshape(slots, targets.shape[0])).astype(BF16)
+    out_ref[...] = dot_n(take_ref[...], returned[...].reshape(slots, total)).astype(BF16)
 
 
 def narrow(pixels, labels, targets):

time: 56.9 us -> 54.8 us (0.963)
  Pallas kernels: 52.5 us -> 50.4 us
    pallas_call x1, Pallas kernels: 52.5 us -> 50.4 us  [narrow(): pl.pallas_call(functools.partial(step_body, bands, owned, n_tile, n_grp),...]
where the time goes in v4:
time: 54.8 us; the launch traced here: 54.6 us
  Pallas kernels  50.4 us (92%)
  local copies, waits for them, and re-layouts  4.21 us (8%)
    pallas_call x1, Pallas kernels, narrow(): pl.pallas_call(functools.partial(step_body, bands, owned, n_tile, n_grp),...  50.4 us
    unnamed x5, local copies, waits for them, and re-layouts  4.21 us

profile of v4, /device:TPU:27, one launch (start us, length us, event | category | flops | bytes accessed | tf_op | source)
XLA Modules:
  0.0 54.6 jit_solution(9593991461954404745)
XLA Ops:
  0.0 0.0 copy-start
  0.0 1.7 %copy.5.tgt_ref = bf16[128,432]{1,0:T(8,128)(2,1)} copy(bf16[128,432]{0,1:T(8,128)(2,1)} %param.5) | data formatting | bytes 221184 | tf_op args[2]
  1.7 0.0 copy-done
  1.7 0.8 %copy.4.pix_ref = bf16[256,432]{1,0:T(8,128)(2,1)} copy(bf16[256,432]{0,1:T(8,128)(2,1)S(1)} %copy-done) | data formatting | bytes 442368 | tf_op args[0]
  2.5 50.4 %shard_map.37 = bf16[256,512]{1,0:T(8,128)(2,1)} custom-call(s32[1,256]{1,0:T(1,128)} %bitcast.1, bf16[256,432]{1,0:T(8,128)(2,1)} %copy.4.pix_ref, bf16[128,432]{1,0:T(8,128)(2,1)} %copy.5.tgt_ref), custom_call_target="tpu_custom_call" | custom-call | tf_op jit(solution)/shard_map/pallas_call | solution.py:298
  52.9 1.7 %copy.7 = bf16[256,512]{1,0:T(8,128)(2,1)} copy(bf16[256,512]{1,0:T(8,128)(2,1)} %shard_map.37) | data formatting | bytes 524288
Async XLA Ops:
  0.0 1.7 %copy-start = (bf16[256,432]{0,1:T(8,128)(2,1)S(1)}, bf16[256,432]{0,1:T(8,128)(2,1)}, u32[]{:S(2)}) copy-start(bf16[256,432]{0,1:T(8,128)(2,1)} %param.3) | copy-start | bytes 663556
